TPU v7x, 32 devices: a whole 2x2x4 slice. The times are simulated.
32 devices in a mesh: dp: 8 (over y, x, core), tensor: 4 (over z).
Axes of the slice: x: 2, y: 2, z: 4, core: 2. Of those that a mesh axis runs over, the one named last changes fastest.
Arguments:
- teacher_input: bfloat16 [8, 1024, 1280], P('dp', 'tensor'), may hold values from -6 to 6
- teacher_upstream: bfloat16 [8, 1024, 1280], P('dp', 'tensor'), may hold values from -6 to 6
- teacher_attn_gain: bfloat16 [1280], P('dp'), may hold values from 0.25 to 1.75
- teacher_attn_shift: bfloat16 [1280], P('dp'), may hold values from -1.75 to 1.75
- teacher_qkv_weight: bfloat16 [3, 1280, 1536], P(None, 'dp', 'tensor'), may hold values from -0.15625 to 0.15625
- teacher_qv_bias: bfloat16 [2, 1536], P(None, 'tensor'), may hold values from -0.625 to 0.625
- teacher_out_weight: bfloat16 [1536, 1280], P('tensor', 'dp'), may hold values from -1.25 to 1.25
- teacher_out_bias: bfloat16 [1280], P('dp'), may hold values from -1.75 to 1.75
- teacher_mlp_gain: bfloat16 [1280], P('dp'), may hold values from 0.25 to 1.75
- teacher_mlp_shift: bfloat16 [1280], P('dp'), may hold values from -1.75 to 1.75
- teacher_fc_weight: bfloat16 [1280, 5120], P('dp', 'tensor'), may hold values from -0.15625 to 0.15625
- teacher_fc_bias: bfloat16 [5120], P('tensor'), may hold values from -1.75 to 1.75
- teacher_proj_weight: bfloat16 [5120, 1280], P('tensor', 'dp'), may hold values from -0.078125 to 0.078125
- teacher_proj_bias: bfloat16 [1280], P('dp'), may hold values from -1.75 to 1.75
- student_input: bfloat16 [8, 1024, 768], P('dp', 'tensor'), may hold values from -6 to 6
- student_upstream: bfloat16 [8, 1024, 768], P('dp', 'tensor'), may hold values from -6 to 6
- student_attn_gain: bfloat16 [768], P('dp'), may hold values from 0.25 to 1.75
- student_attn_shift: bfloat16 [768], P('dp'), may hold values from -1.75 to 1.75
- student_qkv_weight: bfloat16 [3, 768, 768], P(None, 'dp', 'tensor'), may hold values from -0.21875 to 0.21875
- student_qv_bias: bfloat16 [2, 768], P(None, 'tensor'), may hold values from -0.625 to 0.625
- student_out_weight: bfloat16 [768, 768], P('tensor', 'dp'), may hold values from -1.75 to 1.75
- student_out_bias: bfloat16 [768], P('dp'), may hold values from -1.75 to 1.75
- student_mlp_gain: bfloat16 [768], P('dp'), may hold values from 0.25 to 1.75
- student_mlp_shift: bfloat16 [768], P('dp'), may hold values from -1.75 to 1.75
- student_fc_weight: bfloat16 [768, 3072], P('dp', 'tensor'), may hold values from -0.21875 to 0.21875
- student_fc_bias: bfloat16 [3072], P('tensor'), may hold values from -1.75 to 1.75
- student_proj_weight: bfloat16 [3072, 768], P('tensor', 'dp'), may hold values from -0.109375 to 0.109375
- student_proj_bias: bfloat16 [768], P('dp'), may hold values from -1.75 to 1.75
- span_starts: int32 [8], P('dp'), may hold values from 0 to 768, as said below
- head_slots: int32 [24], P('tensor'), may hold values from 0 to 1, as said below
Outputs:
- teacher_output: bfloat16 [8, 1024, 1280], P('dp', 'tensor')
- teacher_input_grad: bfloat16 [8, 1024, 1280], P('dp', 'tensor')
- teacher_attn_gain_grad: float32 [1280], P('dp')
- teacher_attn_shift_grad: float32 [1280], P('dp')
- teacher_qkv_weight_grad: float32 [3, 1280, 1536], P(None, 'dp', 'tensor')
- teacher_qv_bias_grad: float32 [2, 1536], P(None, 'tensor')
- teacher_out_weight_grad: float32 [1536, 1280], P('tensor', 'dp')
- teacher_out_bias_grad: float32 [1280], P('dp')
- teacher_mlp_gain_grad: float32 [1280], P('dp')
- teacher_mlp_shift_grad: float32 [1280], P('dp')
- teacher_fc_weight_grad: float32 [1280, 5120], P('dp', 'tensor')
- teacher_fc_bias_grad: float32 [5120], P('tensor')
- teacher_proj_weight_grad: float32 [5120, 1280], P('tensor', 'dp')
- teacher_proj_bias_grad: float32 [1280], P('dp')
- student_output: bfloat16 [8, 1024, 768], P('dp', 'tensor')
- student_input_grad: bfloat16 [8, 1024, 768], P('dp', 'tensor')
- student_attn_gain_grad: float32 [768], P('dp')
- student_attn_shift_grad: float32 [768], P('dp')
- student_qkv_weight_grad: float32 [3, 768, 768], P(None, 'dp', 'tensor')
- student_qv_bias_grad: float32 [2, 768], P(None, 'tensor')
- student_out_weight_grad: float32 [768, 768], P('tensor', 'dp')
- student_out_bias_grad: float32 [768], P('dp')
- student_mlp_gain_grad: float32 [768], P('dp')
- student_mlp_shift_grad: float32 [768], P('dp')
- student_fc_weight_grad: float32 [768, 3072], P('dp', 'tensor')
- student_fc_bias_grad: float32 [3072], P('tensor')
- student_proj_weight_grad: float32 [3072, 768], P('tensor', 'dp')
- student_proj_bias_grad: float32 [768], P('dp')
Inputs may be any that keep to these rules, and one draw needn't show every extreme that they name: `span_starts`: some sequence starts its span at 0 and some at 768. `head_slots`: exactly 20 of the 24 slots are 1.
All inputs are finite; a program needn't handle non-finite values.
Results may differ from a plain program's by a relative error of at most 0.02.
Values may be sent and summed in bfloat16 or wider, within the bound.
No kernel may reach another device: no remote copies, remote signals or barrier semaphores. Data moves between devices by JAX's collectives and lax.ppermute only.
A program may use at most 256 MiB of HBM per device.

v0:
```python
import jax
import jax.numpy as jnp
from jax import lax
from jax.sharding import PartitionSpec as P

HD = 64
SPAN = 256
epsilon = 1e-05
negative = -1e30


def layer_norm(values, norm_gain, norm_shift):
    center = values - jnp.mean(values, axis=-1, keepdims=True)
    spread = jnp.mean(center * center, axis=-1, keepdims=True)
    return center * lax.rsqrt(spread + epsilon) * norm_gain + norm_shift


def gelu_tanh(values):
    return jax.nn.gelu(values, approximate=True)


def visibility(first_row, block_rows, length, span_start):
    query_pos = first_row + jnp.arange(block_rows, dtype=jnp.int32)
    key_pos = jnp.arange(length, dtype=jnp.int32)
    query_in = (query_pos >= span_start) & (query_pos < span_start + SPAN)
    key_in = (key_pos >= span_start) & (key_pos < span_start + SPAN)
    return (key_pos[None, :] <= query_pos[:, None]) | query_in[:, None] & key_in[None, :]


def block_scores(query_block, key_rows, visible, score_scale):
    scores = (
        jnp.einsum("qhe,khe->hqk", query_block, key_rows, preferred_element_type=jnp.float32)
        * score_scale
    )
    return jnp.where(visible[None], scores, negative)


def attention_forward(query_rows, key_rows, value_rows, span_start, block_rows, score_scale):
    length = query_rows.shape[0]
    results = []
    log_sums = []
    for block_index in range(length // block_rows):
        first_row = block_index * block_rows
        visible = visibility(first_row, block_rows, length, span_start)
        scores = block_scores(
            query_rows[first_row : first_row + block_rows], key_rows, visible, score_scale
        )
        row_peak = jnp.max(scores, axis=-1, keepdims=True)
        raised = jnp.exp(scores - row_peak)
        row_total = jnp.sum(raised, axis=-1, keepdims=True)
        weights = (raised / row_total).astype(jnp.bfloat16)
        results.append(
            jnp.einsum("hqk,khe->qhe", weights, value_rows, preferred_element_type=jnp.float32)
        )
        log_sums.append(row_peak + jnp.log(row_total))
    return (jnp.concatenate(results, axis=0), log_sums)


def attention_backward(
    query_rows, key_rows, value_rows, log_sums, heads_grad, span_start, block_rows, score_scale
):
    length = query_rows.shape[0]
    query_grads = []
    key_grad = jnp.zeros(key_rows.shape, jnp.float32)
    value_grad = jnp.zeros(value_rows.shape, jnp.float32)
    for block_index in range(length // block_rows):
        first_row = block_index * block_rows
        last_row = first_row + block_rows
        visible = visibility(first_row, block_rows, length, span_start)
        scores = block_scores(query_rows[first_row:last_row], key_rows, visible, score_scale)
        probability = jnp.exp(scores - log_sums[block_index])
        grad_block = heads_grad[first_row:last_row]
        value_grad = value_grad + jnp.einsum(
            "hqk,qhe->khe",
            probability.astype(jnp.bfloat16),
            grad_block,
            preferred_element_type=jnp.float32,
        )
        prob_grad = jnp.einsum(
            "qhe,khe->hqk", grad_block, value_rows, preferred_element_type=jnp.float32
        )
        weighted = jnp.sum(probability * prob_grad, axis=-1, keepdims=True)
        score_grad = (probability * (prob_grad - weighted)).astype(jnp.bfloat16)
        query_grads.append(
            jnp.einsum("hqk,khe->qhe", score_grad, key_rows, preferred_element_type=jnp.float32)
            * score_scale
        )
        key_grad = (
            key_grad
            + jnp.einsum(
                "hqk,qhe->khe",
                score_grad,
                query_rows[first_row:last_row],
                preferred_element_type=jnp.float32,
            )
            * score_scale
        )
    return (jnp.concatenate(query_grads, axis=0), key_grad, value_grad)


def gather_rows(normed):
    return lax.all_gather(normed, "tensor", axis=0, tiled=True)


def gather_grads(branch_grad):
    return lax.all_gather(branch_grad, "tensor", axis=0, tiled=True)


def sum_rows(left_rows, right_weight):
    return lax.psum_scatter(
        jnp.dot(left_rows, right_weight, preferred_element_type=jnp.float32).astype(jnp.bfloat16),
        "tensor",
        scatter_dimension=0,
        tiled=True,
    ).astype(jnp.float32)


def back_rows(grad_stack, weight_stack):
    return lax.psum_scatter(
        jnp.einsum(
            "sle,sde->ld", grad_stack, weight_stack, preferred_element_type=jnp.float32
        ).astype(jnp.bfloat16),
        "tensor",
        scatter_dimension=0,
        tiled=True,
    ).astype(jnp.float32)


def run_block(
    inputs,
    upstream,
    attn_gain,
    attn_shift,
    qkv_weight,
    qv_bias,
    out_weight,
    out_bias,
    mlp_gain,
    mlp_shift,
    fc_weight,
    fc_bias,
    proj_weight,
    proj_bias,
    span_start,
    head_keep,
):
    gathered = (
        lax.all_gather(qkv_weight, "dp", axis=1, tiled=True),
        lax.all_gather(out_weight, "dp", axis=1, tiled=True),
        lax.all_gather(fc_weight, "dp", axis=0, tiled=True),
        lax.all_gather(proj_weight, "dp", axis=1, tiled=True),
        lax.all_gather(attn_gain, "dp", axis=0, tiled=True),
        lax.all_gather(attn_shift, "dp", axis=0, tiled=True),
        lax.all_gather(out_bias, "dp", axis=0, tiled=True),
        lax.all_gather(mlp_gain, "dp", axis=0, tiled=True),
        lax.all_gather(mlp_shift, "dp", axis=0, tiled=True),
        lax.all_gather(proj_bias, "dp", axis=0, tiled=True),
    )
    qkv_full, out_full, fc_full, proj_full = (gathered[0], gathered[1], gathered[2], gathered[3])
    gain_one = gathered[4].astype(jnp.float32)
    shift_one = gathered[5].astype(jnp.float32)
    bias_out = gathered[6].astype(jnp.float32)
    gain_two = gathered[7].astype(jnp.float32)
    shift_two = gathered[8].astype(jnp.float32)
    bias_proj = gathered[9].astype(jnp.float32)
    rows_first = inputs[0].astype(jnp.float32)
    normed, norm_back_one = jax.vjp(layer_norm, rows_first, gain_one, shift_one)
    normed_all = gather_rows(normed.astype(jnp.bfloat16))
    projected = jnp.einsum("ld,tde->tle", normed_all, qkv_full, preferred_element_type=jnp.float32)
    bias_pair = qv_bias.astype(jnp.float32)
    length = normed_all.shape[0]
    head_count = head_keep.shape[0]
    head_split = (length, head_count, HD)
    query_rows = (projected[0] + bias_pair[0]).astype(jnp.bfloat16).reshape(head_split)
    key_rows = projected[1].astype(jnp.bfloat16).reshape(head_split)
    value_rows = (projected[2] + bias_pair[1]).astype(jnp.bfloat16).reshape(head_split)
    block_rows = min(512, length)
    score_scale = 1.0 / HD**0.5
    attended, log_sums = attention_forward(
        query_rows, key_rows, value_rows, span_start, block_rows, score_scale
    )
    keep_float = head_keep.astype(jnp.float32)[None, :, None]
    heads_low = (attended * keep_float).astype(jnp.bfloat16).reshape(length, head_count * HD)
    attn_sum = sum_rows(heads_low, out_full)
    middle = rows_first + (attn_sum + bias_out)
    normed_two, norm_back_two = jax.vjp(layer_norm, middle, gain_two, shift_two)
    normed_two_all = gather_rows(normed_two.astype(jnp.bfloat16))
    hidden_pre = jnp.dot(
        normed_two_all, fc_full, preferred_element_type=jnp.float32
    ) + fc_bias.astype(jnp.float32)
    hidden, gelu_back = jax.vjp(gelu_tanh, hidden_pre)
    hidden_low = hidden.astype(jnp.bfloat16)
    mlp_sum = sum_rows(hidden_low, proj_full)
    result = middle + (mlp_sum + bias_proj)
    outputs = result.astype(jnp.bfloat16)[None]
    grad_result = upstream[0].astype(jnp.float32)
    grad_mlp_all = gather_grads(upstream[0])
    proj_bias_grad = jnp.sum(grad_mlp_all, axis=0, dtype=jnp.float32)
    proj_grad = jnp.einsum(
        "lf,ld->fd", hidden_low, grad_mlp_all, preferred_element_type=jnp.float32
    )
    hidden_grad = jnp.einsum(
        "ld,fd->lf", grad_mlp_all, proj_full, preferred_element_type=jnp.float32
    )
    pre_grad = gelu_back(hidden_grad)[0].astype(jnp.bfloat16)
    fc_bias_grad = jnp.sum(pre_grad, axis=0, dtype=jnp.float32)
    fc_grad = jnp.einsum("ld,lf->df", normed_two_all, pre_grad, preferred_element_type=jnp.float32)
    normed_two_grad = back_rows(pre_grad[None], fc_full[None])
    middle_from_norm, gain_two_grad, shift_two_grad = norm_back_two(normed_two_grad)
    middle_grad = grad_result + middle_from_norm
    grad_attn_all = gather_grads(middle_grad.astype(jnp.bfloat16))
    out_bias_grad = jnp.sum(grad_attn_all, axis=0, dtype=jnp.float32)
    out_grad = jnp.einsum("le,ld->ed", heads_low, grad_attn_all, preferred_element_type=jnp.float32)
    heads_grad = (
        jnp.einsum("ld,ed->le", grad_attn_all, out_full, preferred_element_type=jnp.float32)
        .astype(jnp.bfloat16)
        .reshape(head_split)
    )
    heads_grad = heads_grad * head_keep.astype(jnp.bfloat16)[None, :, None]
    query_grad, key_grad, value_grad = attention_backward(
        query_rows, key_rows, value_rows, log_sums, heads_grad, span_start, block_rows, score_scale
    )
    qkv_low = jnp.stack(
        [
            query_grad.reshape(length, head_count * HD),
            key_grad.reshape(length, head_count * HD),
            value_grad.reshape(length, head_count * HD),
        ]
    ).astype(jnp.bfloat16)
    qv_bias_grad = jnp.stack(
        [
            jnp.sum(qkv_low[0], axis=0, dtype=jnp.float32),
            jnp.sum(qkv_low[2], axis=0, dtype=jnp.float32),
        ]
    )
    qkv_grad = jnp.einsum("ld,tle->tde", normed_all, qkv_low, preferred_element_type=jnp.float32)
    normed_grad = back_rows(qkv_low, qkv_full)
    rows_from_norm, gain_one_grad, shift_one_grad = norm_back_one(normed_grad)
    input_grad = (middle_grad + rows_from_norm).astype(jnp.bfloat16)[None]
    norm_sums = lax.psum((gain_one_grad, shift_one_grad, gain_two_grad, shift_two_grad), "tensor")
    matrices = (
        qkv_grad,
        out_grad,
        fc_grad,
        proj_grad,
        norm_sums[0],
        norm_sums[1],
        out_bias_grad,
        norm_sums[2],
        norm_sums[3],
        proj_bias_grad,
    )
    biases = (qv_bias_grad, fc_bias_grad)
    return (outputs, input_grad, matrices, biases)


def arrange(outputs, input_grad, matrices, biases):
    return (
        outputs,
        input_grad,
        matrices[4],
        matrices[5],
        matrices[0],
        biases[0],
        matrices[1],
        matrices[6],
        matrices[7],
        matrices[8],
        matrices[2],
        biases[1],
        matrices[3],
        matrices[9],
    )


def on_device(
    teacher_input,
    teacher_upstream,
    teacher_attn_gain,
    teacher_attn_shift,
    teacher_qkv_weight,
    teacher_qv_bias,
    teacher_out_weight,
    teacher_out_bias,
    teacher_mlp_gain,
    teacher_mlp_shift,
    teacher_fc_weight,
    teacher_fc_bias,
    teacher_proj_weight,
    teacher_proj_bias,
    student_input,
    student_upstream,
    student_attn_gain,
    student_attn_shift,
    student_qkv_weight,
    student_qv_bias,
    student_out_weight,
    student_out_bias,
    student_mlp_gain,
    student_mlp_shift,
    student_fc_weight,
    student_fc_bias,
    student_proj_weight,
    student_proj_bias,
    span_starts,
    head_slots,
):
    span_start = span_starts[0]
    teacher = run_block(
        teacher_input,
        teacher_upstream,
        teacher_attn_gain,
        teacher_attn_shift,
        teacher_qkv_weight,
        teacher_qv_bias,
        teacher_out_weight,
        teacher_out_bias,
        teacher_mlp_gain,
        teacher_mlp_shift,
        teacher_fc_weight,
        teacher_fc_bias,
        teacher_proj_weight,
        teacher_proj_bias,
        span_start,
        head_slots,
    )
    student_keep = jnp.ones((student_qv_bias.shape[1] // HD,), jnp.int32)
    student = run_block(
        student_input,
        student_upstream,
        student_attn_gain,
        student_attn_shift,
        student_qkv_weight,
        student_qv_bias,
        student_out_weight,
        student_out_bias,
        student_mlp_gain,
        student_mlp_shift,
        student_fc_weight,
        student_fc_bias,
        student_proj_weight,
        student_proj_bias,
        span_start,
        student_keep,
    )
    teach_parts = teacher[2]
    learn_parts = student[2]
    summed = (
        lax.psum_scatter(teach_parts[0], "dp", scatter_dimension=1, tiled=True),
        lax.psum_scatter(teach_parts[1], "dp", scatter_dimension=1, tiled=True),
        lax.psum_scatter(teach_parts[2], "dp", scatter_dimension=0, tiled=True),
        lax.psum_scatter(teach_parts[3], "dp", scatter_dimension=1, tiled=True),
        lax.psum_scatter(teach_parts[4], "dp", scatter_dimension=0, tiled=True),
        lax.psum_scatter(teach_parts[5], "dp", scatter_dimension=0, tiled=True),
        lax.psum_scatter(teach_parts[6], "dp", scatter_dimension=0, tiled=True),
        lax.psum_scatter(teach_parts[7], "dp", scatter_dimension=0, tiled=True),
        lax.psum_scatter(teach_parts[8], "dp", scatter_dimension=0, tiled=True),
        lax.psum_scatter(teach_parts[9], "dp", scatter_dimension=0, tiled=True),
        lax.psum_scatter(learn_parts[0], "dp", scatter_dimension=1, tiled=True),
        lax.psum_scatter(learn_parts[1], "dp", scatter_dimension=1, tiled=True),
        lax.psum_scatter(learn_parts[2], "dp", scatter_dimension=0, tiled=True),
        lax.psum_scatter(learn_parts[3], "dp", scatter_dimension=1, tiled=True),
        lax.psum_scatter(learn_parts[4], "dp", scatter_dimension=0, tiled=True),
        lax.psum_scatter(learn_parts[5], "dp", scatter_dimension=0, tiled=True),
        lax.psum_scatter(learn_parts[6], "dp", scatter_dimension=0, tiled=True),
        lax.psum_scatter(learn_parts[7], "dp", scatter_dimension=0, tiled=True),
        lax.psum_scatter(learn_parts[8], "dp", scatter_dimension=0, tiled=True),
        lax.psum_scatter(learn_parts[9], "dp", scatter_dimension=0, tiled=True),
    )
    totals = lax.psum((teacher[3][0], teacher[3][1], student[3][0], student[3][1]), "dp")
    teacher_matrices = summed[0:10]
    student_matrices = summed[10:20]
    teacher_biases = (totals[0], totals[1])
    student_biases = (totals[2], totals[3])
    return arrange(teacher[0], teacher[1], teacher_matrices, teacher_biases) + arrange(
        student[0], student[1], student_matrices, student_biases
    )


def solution(mesh):
    in_specs = (
        P("dp", "tensor", None),
        P("dp", "tensor", None),
        P("dp"),
        P("dp"),
        P(None, "dp", "tensor"),
        P(None, "tensor"),
        P("tensor", "dp"),
        P("dp"),
        P("dp"),
        P("dp"),
        P("dp", "tensor"),
        P("tensor"),
        P("tensor", "dp"),
        P("dp"),
        P("dp", "tensor", None),
        P("dp", "tensor", None),
        P("dp"),
        P("dp"),
        P(None, "dp", "tensor"),
        P(None, "tensor"),
        P("tensor", "dp"),
        P("dp"),
        P("dp"),
        P("dp"),
        P("dp", "tensor"),
        P("tensor"),
        P("tensor", "dp"),
        P("dp"),
        P("dp"),
        P("tensor"),
    )
    out_specs = (
        P("dp", "tensor", None),
        P("dp", "tensor", None),
        P("dp"),
        P("dp"),
        P(None, "dp", "tensor"),
        P(None, "tensor"),
        P("tensor", "dp"),
        P("dp"),
        P("dp"),
        P("dp"),
        P("dp", "tensor"),
        P("tensor"),
        P("tensor", "dp"),
        P("dp"),
        P("dp", "tensor", None),
        P("dp", "tensor", None),
        P("dp"),
        P("dp"),
        P(None, "dp", "tensor"),
        P(None, "tensor"),
        P("tensor", "dp"),
        P("dp"),
        P("dp"),
        P("dp"),
        P("dp", "tensor"),
        P("tensor"),
        P("tensor", "dp"),
        P("dp"),
    )
    return jax.shard_map(
        on_device, mesh=mesh, in_specs=in_specs, out_specs=out_specs, check_vma=False
    )
```

profile of v0, /device:TPU:0, one launch (start us, length us, event | category | flops | bytes accessed | tf_op | source)
XLA Modules:
  0.0 1425.0 jit_solution(5786993439719821327)
XLA Ops:
  22.5 26.5 %all-reduce.27 = (bf16[1280]{0:T(1024)(128)(2,1)}, bf16[1280]{0:T(1024)(128)(2,1)}, bf16[1280]{0:T(1024)(128)(2,1)S(1)}, bf16[1280]{0:T(1024)(128)(2,1)S(1)}, bf...) all-reduce(bf16[1280]{0:T(1024)(128)(2,1)S(1)} %dynamic-update-slic, ...), channel_id=1, replica_groups=mesh['dp'=8,'tensor'=4] {'dp'}, use_global_device_ids=true, to_apply=%add.4 | all-reduce | flops 12288 | bytes 49152
  56.3 10.9 all_gather.88
  67.2 13.4 all_gather.101
  80.7 9.0 all_gather.102
  108.0 35.6 %all-gather.16.cloned.1.call-done = bf16[1024,1280]{1,0:T(8,128)(2,1)} async-done(((bf16[256,1280]{1,0:T(8,128)(2,1)}), bf16[1024,1280]{1,0:T(8,128)(2,1)}) %all-gather.16.cloned.1.call-update) | async-done | bytes 2621456 | tf_op jit(solution)/shard_map/all_gather | solution.py:102
  143.6 32.2 %all-gather.18.cloned.1.call-done = bf16[3,1280,384]{2,1,0:T(8,128)(2,1)} async-done(((bf16[3,160,384]{2,1,0:T(8,128)(2,1)}), bf16[3,1280,384]{2,1,0:T(8,128)(2,1)}) %all-gather.18.cloned.1.call-update) | async-done | bytes 2949136 | tf_op jit(solution)/shard_map/all_gather | solution.py:148
  175.8 6.0 fusion.47
  184.9 3.0 fusion
  189.5 3.8 fusion.10
  195.8 2.8 fusion.1
  200.5 3.8 fusion.11
  205.2 3.2 convolution_convert_fusion
  209.1 4.2 reduce-scatter.34.cloned.1.call-done
  220.0 46.6 %reduce-scatter.20.cloned.1.call-done = bf16[256,1280]{1,0:T(8,128)(2,1)} async-done(((bf16[1024,1280]{1,0:T(8,128)(2,1)}), bf16[256,1280]{1,0:T(8,128)(2,1)}) %reduce-scatter.20.cloned.1.call-update) | async-done | bytes 655376 | tf_op jit(solution)/shard_map/reduce_scatter | solution.py:110
  273.4 18.7 %all-gather.32.cloned.1.call-done = bf16[768,768]{1,0:T(8,128)(2,1)} async-done(((bf16[96,768]{1,0:T(8,128)(2,1)}), bf16[768,768]{1,0:T(8,128)(2,1)}) %all-gather.32.cloned.1.call-update) | async-done | bytes 1179664 | tf_op jit(solution)/shard_map/all_gather | solution.py:150
  292.1 39.3 %all-gather.30.cloned.1.call-done = bf16[1024,768]{1,0:T(8,128)(2,1)} async-done(((bf16[256,768]{1,0:T(8,128)(2,1)}), bf16[1024,768]{1,0:T(8,128)(2,1)}) %all-gather.30.cloned.1.call-update) | async-done | bytes 1572880 | tf_op jit(solution)/shard_map/all_gather | solution.py:102
  331.4 4.8 fusion.170
  336.2 20.0 %all-gather.34.cloned.1.call-done = bf16[768,768]{0,1:T(8,128)(2,1)} async-done(((bf16[768,96]{0,1:T(8,128)(2,1)}), bf16[768,768]{0,1:T(8,128)(2,1)}) %all-gather.34.cloned.1.call-update) | async-done | bytes 1179664 | tf_op jit(solution)/shard_map/all_gather | solution.py:151
  356.2 38.7 %all-gather.40.cloned.1.call-done = bf16[1,1024,768]{2,1,0:T(8,128)(2,1)} async-done(((bf16[1,256,768]{2,1,0:T(8,128)(2,1)}), bf16[1,1024,768]{2,1,0:T(8,128)(2,1)}) %all-gather.40.cloned.1.call-update) | async-done | bytes 1572880 | tf_op jit(solution)/shard_map/all_gather | solution.py:106
  394.9 6.3 convert_reduce_fusion.4
  405.1 5.5 convolution_convert_fusion.4
  411.0 17.4 %all-gather.22.cloned.1.call-done = bf16[1280,1280]{1,0:T(8,128)(2,1)} async-done(((bf16[160,1280]{1,0:T(8,128)(2,1)}), bf16[1280,1280]{1,0:T(8,128)(2,1)}) %all-gather.22.cloned.1.call-update) | async-done | bytes 3276816 | tf_op jit(solution)/shard_map/all_gather | solution.py:150
  428.4 57.0 %all-gather.20.cloned.1.call-done = bf16[1024,1280]{1,0:T(8,128)(2,1)} async-done(((bf16[256,1280]{1,0:T(8,128)(2,1)}), bf16[1024,1280]{1,0:T(8,128)(2,1)}) %all-gather.20.cloned.1.call-update) | async-done | bytes 2621456 | tf_op jit(solution)/shard_map/all_gather | solution.py:102
  485.4 8.6 fusion.166
  493.9 46.5 %all-gather.38.cloned.1.call-done = bf16[1,1024,1280]{2,1,0:T(8,128)(2,1)} async-done(((bf16[1,256,1280]{2,1,0:T(8,128)(2,1)}), bf16[1,1024,1280]{2,1,0:T(8,128)(2,1)}) %all-gather.38.cloned.1.call-update) | async-done | bytes 2621456 | tf_op jit(solution)/shard_map/all_gather | solution.py:106
  540.4 33.6 %all-gather.24.cloned.1.call-done = bf16[1280,1280]{0,1:T(8,128)(2,1)} async-done(((bf16[1280,160]{0,1:T(8,128)(2,1)}), bf16[1280,1280]{0,1:T(8,128)(2,1)}) %all-gather.24.cloned.1.call-update) | async-done | bytes 3276816 | tf_op jit(solution)/shard_map/all_gather | solution.py:151
  574.0 10.7 convert_reduce_fusion.1
  586.2 4.9 convolution_convert_fusion.1
  591.2 9.7 convolution_convert_fusion.2
  601.0 10.4 reduce-scatter.38.cloned.1.call-done
  613.5 34.4 %reduce-scatter.36.cloned.1.call-done = bf16[256,768]{1,0:T(8,128)(2,1)} async-done(((bf16[1024,768]{1,0:T(8,128)(2,1)}), bf16[256,768]{1,0:T(8,128)(2,1)}) %reduce-scatter.36.cloned.1.call-update) | async-done | bytes 393232 | tf_op jit(solution)/shard_map/reduce_scatter | solution.py:110
  652.7 48.5 %reduce-scatter.24.cloned.1.call-done = bf16[256,1280]{1,0:T(8,128)(2,1)} async-done(((bf16[1024,1280]{1,0:T(8,128)(2,1)}), bf16[256,1280]{1,0:T(8,128)(2,1)}) %reduce-scatter.24.cloned.1.call-update) | async-done | bytes 655376 | tf_op jit(solution)/shard_map/reduce_scatter | solution.py:119
  703.5 51.6 %reduce-scatter.22.cloned.1.call-done = bf16[256,1280]{1,0:T(8,128)(2,1)} async-done(((bf16[1024,1280]{1,0:T(8,128)(2,1)}), bf16[256,1280]{1,0:T(8,128)(2,1)}) %reduce-scatter.22.cloned.1.call-update) | async-done | bytes 655376 | tf_op jit(solution)/shard_map/reduce_scatter | solution.py:110
  755.2 2.8 fusion.156
  760.7 33.2 %all-gather.36.cloned.1.call-done = bf16[1024,768]{1,0:T(8,128)(2,1)} async-done(((bf16[256,768]{1,0:T(8,128)(2,1)}), bf16[1024,768]{1,0:T(8,128)(2,1)}) %all-gather.36.cloned.1.call-update) | async-done | bytes 1572880 | tf_op jit(solution)/shard_map/all_gather | solution.py:106
  799.7 4.3 multiply_reduce_fusion.3
  811.9 5.1 multiply_reduce_fusion.2
  817.1 5.6 multiply_convert_fusion.2
  830.1 4.8 reshape.472
  835.0 3.9 bitcast_convert_fusion.1
  839.2 10.6 all-gather.26.cloned.1.call-done
  849.8 3.0 convolution_convert_fusion.6
  853.0 6.0 fusion.4
  859.0 9.6 multiply_reduce_fusion
  868.6 6.2 multiply_reduce_fusion.1
  878.3 9.7 multiply_convert_fusion.1
  892.7 6.9 multiply_convert_fusion
  903.4 5.0 fusion.95
  911.0 8.4 convolution_bitcast_fusion
  919.3 9.8 copy.70
  929.2 7.8 bitcast_convert_fusion
  937.1 5.2 fusion.63
  942.6 4.7 fusion.172
  947.4 9.8 fusion.38
  957.3 8.9 fusion.168
  977.5 5.3 fusion.152
  987.0 105.4 %all-reduce.30.cloned.1.call-done = f32[3,1280,384]{2,0,1:T(4,128)} async-done(((f32[3,1280,384]{2,0,1:T(4,128)}), f32[3,1280,384]{2,0,1:T(4,128)}) %all-reduce.30.cloned.1.call-update) | async-done | bytes 5898256
  1094.7 52.2 %reduce-scatter.26.cloned.1.call-done = bf16[256,1280]{1,0:T(8,128)(2,1)} async-done(((bf16[1024,1280]{1,0:T(8,128)(2,1)}), bf16[256,1280]{1,0:T(8,128)(2,1)}) %reduce-scatter.26.cloned.1.call-update) | async-done | bytes 655376 | tf_op jit(solution)/shard_map/reduce_scatter | solution.py:119
  1150.3 25.6 %all-reduce.25 = (f32[1280]{0:T(1024)S(1)}, f32[1280]{0:T(1024)S(1)}, f32[2,384]{1,0:T(2,128)}, f32[1280]{0:T(1024)S(1)}, f32[1280]{0:T(1024)S(1)}, /*index=5*/f...) all-reduce(f32[1280]{0:T(1024)S(1)} %get-tuple-element.86, ...), channel_id=8, replica_groups=mesh['dp'=8,'tensor'=4] {'dp'}, use_global_device_ids=true, to_apply=%region_20.21.clone | all-reduce | flops 15488 | bytes 123904
  1178.9 11.3 all-reduce.26
  1193.0 46.7 %reduce-scatter.42.cloned.1.call-done = f32[96,768]{1,0:T(8,128)} async-done(((f32[768,768]{1,0:T(8,128)}), f32[96,768]{1,0:T(8,128)}) %reduce-scatter.42.cloned.1.call-update) | async-done | bytes 294928 | tf_op jit(solution)/shard_map/reduce_scatter | solution.py:361
  1239.6 66.9 %reduce-scatter.32.cloned.1.call-done = f32[1280,160]{0,1:T(8,128)} async-done(((f32[1280,1280]{0,1:T(8,128)}), f32[1280,160]{0,1:T(8,128)}) %reduce-scatter.32.cloned.1.call-update) | async-done | bytes 819216 | tf_op jit(solution)/shard_map/reduce_scatter | solution.py:352
  1306.5 67.4 %reduce-scatter.30.cloned.1.call-done = f32[160,1280]{1,0:T(8,128)} async-done(((f32[1280,1280]{1,0:T(8,128)}), f32[160,1280]{1,0:T(8,128)}) %reduce-scatter.30.cloned.1.call-update) | async-done | bytes 819216 | tf_op jit(solution)/shard_map/reduce_scatter | solution.py:351
  1374.0 44.3 %reduce-scatter.28.cloned.1.call-done = f32[384,160]{0,1:T(8,128)} async-done(((f32[384,1280]{0,1:T(8,128)}), f32[384,160]{0,1:T(8,128)}) %reduce-scatter.28.cloned.1.call-update) | async-done | bytes 245776 | tf_op jit(solution)/shard_map/reduce_scatter | solution.py:350
  (509 shorter events, 141.7 us)
Async XLA Ops:
  7.2 45.2 %copy-start.4 = (bf16[1,256,1280]{2,1,0:T(8,128)(2,1)S(1)}, bf16[1,256,1280]{2,1,0:T(8,128)(2,1)}, u32[]{:S(2)}) copy-start(bf16[1,256,1280]{2,1,0:T(8,128)(2,1)} %param.30) | copy-start | bytes 1966084
  7.2 48.2 %copy-start.118 = (s32[6]{0:T(128)S(1)}, s32[6]{0:T(128)}, u32[]{:S(2)}) copy-start(s32[6]{0:T(128)} %param.59) | copy-start | bytes 76
  7.2 48.7 %copy-start.103 = (bf16[2,192]{1,0:T(2,128)(2,1)S(1)}, bf16[2,192]{1,0:T(2,128)(2,1)}, u32[]{:S(2)}) copy-start(bf16[2,192]{1,0:T(2,128)(2,1)} %param.49) | copy-start | bytes 2308
  7.2 48.7 %copy-start.113 = (bf16[2,384]{1,0:T(2,128)(2,1)S(1)}, bf16[2,384]{1,0:T(2,128)(2,1)}, u32[]{:S(2)}) copy-start(bf16[2,384]{1,0:T(2,128)(2,1)} %param.35) | copy-start | bytes 4612
  7.2 48.8 %copy-start.73 = (bf16[192,96]{1,0:T(8,128)(2,1)S(1)}, bf16[192,96]{1,0:T(8,128)(2,1)}, u32[]{:S(2)}) copy-start(bf16[192,96]{1,0:T(8,128)(2,1)} %param.50) | copy-start | bytes 110596
  7.3 48.9 %copy-start.60 = (bf16[3,96,192]{2,1,0:T(8,128)(2,1)S(1)}, bf16[3,96,192]{2,1,0:T(8,128)(2,1)}, u32[]{:S(2)}) copy-start(bf16[3,96,192]{2,1,0:T(8,128)(2,1)} %param.48) | copy-start | bytes 331780
  7.3 85.9 %all-gather.28.cloned.1.call-start = ((), (), s32[]{:S(2)}) async-start(), calls=%async_computation.28 | async-start | bytes 1966080 | tf_op jit(solution)/shard_map/all_gather | solution.py:102
  9.9 46.3 %copy-start.66 = (bf16[384,160]{0,1:T(8,128)(2,1)S(1)}, bf16[384,160]{0,1:T(8,128)(2,1)}, u32[]{:S(2)}) copy-start(bf16[384,160]{0,1:T(8,128)(2,1)} %param.36) | copy-start | bytes 368644
  11.1 56.1 %copy-start.74 = (f32[256]{0:T(256)}, f32[256]{0:T(256)S(1)}, u32[]{:S(2)}) copy-start(f32[256]{0:T(256)S(1)} %broadcast_multiply_fusion.2) | copy-start | bytes 3076
  51.0 92.6 %all-gather.16.cloned.1.call-start = ((), (), s32[]{:S(2)}) async-start(), calls=%async_computation.15 | async-start | bytes 3276800 | tf_op jit(solution)/shard_map/all_gather | solution.py:102
  52.7 39.3 %copy-start.90 = (f32[256]{0:T(256)}, f32[256]{0:T(256)S(1)}, u32[]{:S(2)}) copy-start(f32[256]{0:T(256)S(1)} %fusion.81) | copy-start | bytes 3076
  53.9 121.9 %all-gather.18.cloned.1.call-start = ((), (), s32[]{:S(2)}) async-start(), calls=%async_computation.16 | async-start | bytes 3317760 | tf_op jit(solution)/shard_map/all_gather | solution.py:148
  54.7 158.6 %reduce-scatter.34.cloned.1.call-start = ((), (), s32[]{:S(2)}) async-start(), calls=%async_computation.29 | async-start | bytes 1966080 | tf_op jit(solution)/shard_map/reduce_scatter | solution.py:110
  90.0 114.4 %copy-start.107 = (f32[384]{0:T(512)}, f32[384]{0:T(512)S(1)}, u32[]{:S(2)}) copy-start(f32[384]{0:T(512)S(1)} %mul.401) | copy-start | bytes 4612
  105.6 76.2 %copy-start.55 = (bf16[3,64,512]{2,1,0:T(8,128)(2,1)}, bf16[3,64,512]{2,1,0:T(8,128)(2,1)S(1)}, u32[]{:S(2)}) copy-start(bf16[3,64,512]{2,1,0:T(8,128)(2,1)S(1)} %fusion.100) | copy-start | bytes 589828
  107.5 159.1 %reduce-scatter.20.cloned.1.call-start = ((), (), s32[]{:S(2)}) async-start(), calls=%async_computation.17 | async-start | bytes 3276800 | tf_op jit(solution)/shard_map/reduce_scatter | solution.py:110
  208.4 83.7 %all-gather.32.cloned.1.call-start = ((), (), s32[]{:S(2)}) async-start(), calls=%async_computation.31 | async-start | bytes 1327104 | tf_op jit(solution)/shard_map/all_gather | solution.py:150
  209.0 122.3 %all-gather.30.cloned.1.call-start = ((), (), s32[]{:S(2)}) async-start(), calls=%async_computation.30 | async-start | bytes 1966080 | tf_op jit(solution)/shard_map/all_gather | solution.py:102
  217.8 138.4 %all-gather.34.cloned.1.call-start = ((), (), s32[]{:S(2)}) async-start(), calls=%async_computation.32 | async-start | bytes 1327104 | tf_op jit(solution)/shard_map/all_gather | solution.py:151
  218.6 176.3 %all-gather.40.cloned.1.call-start = ((), (), s32[]{:S(2)}) async-start(), calls=%async_computation.40 | async-start | bytes 1966080 | tf_op jit(solution)/shard_map/all_gather | solution.py:106
  219.3 209.1 %all-gather.22.cloned.1.call-start = ((), (), s32[]{:S(2)}) async-start(), calls=%async_computation.19 | async-start | bytes 3686400 | tf_op jit(solution)/shard_map/all_gather | solution.py:150
  219.9 265.5 %all-gather.20.cloned.1.call-start = ((), (), s32[]{:S(2)}) async-start(), calls=%async_computation.18 | async-start | bytes 3276800 | tf_op jit(solution)/shard_map/all_gather | solution.py:102
  220.0 53.4 %copy-start.106 = (bf16[768]{0:T(1024)(128)(2,1)S(1)}, bf16[768]{0:T(1024)(128)(2,1)}, u32[]{:S(2)}) copy-start(bf16[768]{0:T(1024)(128)(2,1)} %param.55) | copy-start | bytes 4612
  271.8 268.6 %all-gather.38.cloned.1.call-start = ((), (), s32[]{:S(2)}) async-start(), calls=%async_computation.39 | async-start | bytes 3276800 | tf_op jit(solution)/shard_map/all_gather | solution.py:106
  272.4 301.6 %all-gather.24.cloned.1.call-start = ((), (), s32[]{:S(2)}) async-start(), calls=%async_computation.20 | async-start | bytes 3686400 | tf_op jit(solution)/shard_map/all_gather | solution.py:151
  273.1 338.3 %reduce-scatter.38.cloned.1.call-start = ((), (), s32[]{:S(2)}) async-start(), calls=%async_computation.34 | async-start | bytes 1966080 | tf_op jit(solution)/shard_map/reduce_scatter | solution.py:119
  273.4 131.6 %copy-start.104 = (f32[768]{0:T(1024)}, f32[768]{0:T(1024)S(1)}, u32[]{:S(2)}) copy-start(f32[768]{0:T(1024)S(1)} %convert_element_type.331) | copy-start | bytes 9220
  336.2 66.2 %copy-start.117 = (bf16[768,768]{1,0:T(8,128)(2,1)S(1)}, bf16[768,768]{1,0:T(8,128)(2,1)}, u32[]{:S(2)}) copy-start(bf16[768,768]{1,0:T(8,128)(2,1)} %all-gather.32.cloned.1.call-done) | copy-start | bytes 3538948
  405.0 242.9 %reduce-scatter.36.cloned.1.call-start = ((), (), s32[]{:S(2)}) async-start(), calls=%async_computation.33 | async-start | bytes 1966080 | tf_op jit(solution)/shard_map/reduce_scatter | solution.py:110
  410.5 290.6 %reduce-scatter.24.cloned.1.call-start = ((), (), s32[]{:S(2)}) async-start(), calls=%async_computation.22 | async-start | bytes 3276800 | tf_op jit(solution)/shard_map/reduce_scatter | solution.py:119
  411.0 180.2 %copy-start.95 = (f32[1280]{0:T(1024)}, f32[1280]{0:T(1024)S(1)}, u32[]{:S(2)}) copy-start(f32[1280]{0:T(1024)S(1)} %convert_element_type.289) | copy-start | bytes 15364
  591.1 164.0 %reduce-scatter.22.cloned.1.call-start = ((), (), s32[]{:S(2)}) async-start(), calls=%async_computation.21 | async-start | bytes 3276800 | tf_op jit(solution)/shard_map/reduce_scatter | solution.py:110
  600.9 51.7 %copy-start.99 = (bf16[1280]{0:T(1024)(128)(2,1)S(1)}, bf16[1280]{0:T(1024)(128)(2,1)}, u32[]{:S(2)}) copy-start(bf16[1280]{0:T(1024)(128)(2,1)} %get-tuple-element.129) | copy-start | bytes 7684
  601.0 100.2 %copy-start.11 = (bf16[256,1280]{1,0:T(8,128)(2,1)S(1)}, bf16[256,1280]{1,0:T(8,128)(2,1)}, u32[]{:S(2)}) copy-start(bf16[256,1280]{1,0:T(8,128)(2,1)} %reduce-scatter.20.cloned.1.call-done) | copy-start | bytes 1966084
  601.0 193.0 %all-gather.36.cloned.1.call-start = ((), (), s32[]{:S(2)}) async-start(), calls=%async_computation.35 | async-start | bytes 1966080 | tf_op jit(solution)/shard_map/all_gather | solution.py:106
  650.2 53.3 %copy-start.23 = (f32[256,768]{1,0:T(8,128)}, f32[256,768]{1,0:T(8,128)S(1)}, u32[]{:S(2)}) copy-start(f32[256,768]{1,0:T(8,128)S(1)} %get-tuple-element.137) | copy-start | bytes 2359300
  650.2 107.8 %copy-start.92 = (f32[256]{0:T(256)}, f32[256]{0:T(256)S(1)}, u32[]{:S(2)}) copy-start(f32[256]{0:T(256)S(1)} %negate_multiply_fusion.1) | copy-start | bytes 3076
  652.4 197.4 %all-gather.26.cloned.1.call-start = ((), (), s32[]{:S(2)}) async-start(), calls=%async_computation.23 | async-start | bytes 3276800 | tf_op jit(solution)/shard_map/all_gather | solution.py:106
  760.6 211.8 %reduce-scatter.48.cloned.1.call-start = ((), (), s32[]{:S(2)}) async-start(), calls=%async_computation.42 | async-start | bytes 884736
  760.7 49.1 %copy-start.65 = (f32[3,512]{1,0:T(4,128)}, f32[3,512]{1,0:T(4,128)S(1)}, u32[]{:S(2)}) copy-start(f32[3,512]{1,0:T(4,128)S(1)} %log_add_fusion.2) | copy-start | bytes 18436
  760.7 43.2 %copy-start.63 = (f32[3,512]{1,0:T(4,128)}, f32[3,512]{1,0:T(4,128)S(1)}, u32[]{:S(2)}) copy-start(f32[3,512]{1,0:T(4,128)S(1)} %log_add_fusion.3) | copy-start | bytes 18436
  817.0 157.1 %reduce-scatter.46.cloned.1.call-start = ((), (), s32[]{:S(2)}) async-start(), calls=%async_computation.41 | async-start | bytes 2211840
  834.9 141.0 %reduce-scatter.40.cloned.1.call-start = ((), (), s32[]{:S(2)}) async-start(), calls=%async_computation.36 | async-start | bytes 1966080 | tf_op jit(solution)/shard_map/reduce_scatter | solution.py:119
  838.9 253.5 %all-reduce.30.cloned.1.call-start = ((), (), s32[]{:S(2)}) async-start(), calls=%async_computation.43 | async-start | bytes 15728640
  929.2 217.7 %reduce-scatter.26.cloned.1.call-start = ((), (), s32[]{:S(2)}) async-start(), calls=%async_computation.24 | async-start | bytes 3276800 | tf_op jit(solution)/shard_map/reduce_scatter | solution.py:119
  937.0 255.9 %reduce-scatter.44.cloned.1.call-start = ((), (), s32[]{:S(2)}) async-start(), calls=%async_computation.38 | async-start | bytes 2654208 | tf_op jit(solution)/shard_map/reduce_scatter | solution.py:362
  942.4 297.3 %reduce-scatter.42.cloned.1.call-start = ((), (), s32[]{:S(2)}) async-start(), calls=%async_computation.37 | async-start | bytes 2654208 | tf_op jit(solution)/shard_map/reduce_scatter | solution.py:361
  947.3 359.2 %reduce-scatter.32.cloned.1.call-start = ((), (), s32[]{:S(2)}) async-start(), calls=%async_computation.27 | async-start | bytes 7372800 | tf_op jit(solution)/shard_map/reduce_scatter | solution.py:352
  957.2 416.7 %reduce-scatter.30.cloned.1.call-start = ((), (), s32[]{:S(2)}) async-start(), calls=%async_computation.26 | async-start | bytes 7372800 | tf_op jit(solution)/shard_map/reduce_scatter | solution.py:351
  966.2 452.1 %reduce-scatter.28.cloned.1.call-start = ((), (), s32[]{:S(2)}) async-start(), calls=%async_computation.25 | async-start | bytes 2211840 | tf_op jit(solution)/shard_map/reduce_scatter | solution.py:350
  986.4 160.4 %copy-start.59 = (f32[1280]{0:T(1024)S(1)}, f32[1280]{0:T(1024)}, u32[]{:S(2)}) copy-start(f32[1280]{0:T(1024)} %copy-done.58) | copy-start | bytes 15364
  986.4 160.4 %copy-start.77 = (f32[256]{0:T(256)S(1)}, f32[256]{0:T(256)}, u32[]{:S(2)}) copy-start(f32[256]{0:T(256)} %copy-done.76) | copy-start | bytes 3076
  986.9 161.6 %copy-start.91 = (f32[256]{0:T(256)S(1)}, f32[256]{0:T(256)}, u32[]{:S(2)}) copy-start(f32[256]{0:T(256)} %copy-done.90) | copy-start | bytes 3076
  986.9 161.6 %copy-start.85 = (f32[256]{0:T(256)S(1)}, f32[256]{0:T(256)}, u32[]{:S(2)}) copy-start(f32[256]{0:T(256)} %copy-done.84) | copy-start | bytes 3076
  986.9 163.4 %copy-start.78 = (f32[1280]{0:T(1024)S(1)}, f32[1280]{0:T(1024)}, u32[]{:S(2)}) copy-start(f32[1280]{0:T(1024)} %get-tuple-element.84) | copy-start | bytes 15364
  986.9 163.4 %copy-start.79 = (f32[1280]{0:T(1024)S(1)}, f32[1280]{0:T(1024)}, u32[]{:S(2)}) copy-start(f32[1280]{0:T(1024)} %get-tuple-element.92) | copy-start | bytes 15364
  986.9 163.4 %copy-start.82 = (f32[768]{0:T(1024)S(1)}, f32[768]{0:T(1024)}, u32[]{:S(2)}) copy-start(f32[768]{0:T(1024)} %get-tuple-element.88) | copy-start | bytes 9220
  986.9 163.4 %copy-start.83 = (f32[768]{0:T(1024)S(1)}, f32[768]{0:T(1024)}, u32[]{:S(2)}) copy-start(f32[768]{0:T(1024)} %get-tuple-element.95) | copy-start | bytes 9220
  986.9 163.4 %copy-start.94 = (f32[1280]{0:T(1024)S(1)}, f32[1280]{0:T(1024)}, u32[]{:S(2)}) copy-start(f32[1280]{0:T(1024)} %get-tuple-element.162) | copy-start | bytes 15364
  986.9 163.4 %copy-start.98 = (f32[768]{0:T(1024)S(1)}, f32[768]{0:T(1024)}, u32[]{:S(2)}) copy-start(f32[768]{0:T(1024)} %get-tuple-element.172) | copy-start | bytes 9220
  987.0 203.3 %copy-start.15 = (f32[256,1280]{1,0:T(8,128)S(1)}, f32[256,1280]{1,0:T(8,128)}, u32[]{:S(2)}) copy-start(f32[256,1280]{1,0:T(8,128)} %copy-done.14) | copy-start | bytes 3932164
  987.0 203.3 %copy-start.24 = (bf16[1,256,1280]{2,1,0:T(8,128)(2,1)S(1)}, bf16[1,256,1280]{2,1,0:T(8,128)(2,1)}, u32[]{:S(2)}) copy-start(bf16[1,256,1280]{2,1,0:T(8,128)(2,1)} %param.31) | copy-start | bytes 1966084
  987.0 203.3 %copy-start.87 = (f32[256]{0:T(256)S(1)}, f32[256]{0:T(256)}, u32[]{:S(2)}) copy-start(f32[256]{0:T(256)} %copy-done.86) | copy-start | bytes 3076
  1146.9 43.4 %copy-start.25 = (bf16[256,1280]{1,0:T(8,128)(2,1)S(1)}, bf16[256,1280]{1,0:T(8,128)(2,1)}, u32[]{:S(2)}) copy-start(bf16[256,1280]{1,0:T(8,128)(2,1)} %reduce-scatter.26.cloned.1.call-done) | copy-start | bytes 1966084
  (100 other events, 846.7 us)
Sparse Core Ops, SparseCore 0:
  51.1 36.5 all-gather.27
  89.9 53.6 all-gather.15
  145.5 30.2 all-gather.17
  178.0 35.2 reduce-scatter.33
  215.5 51.0 reduce-scatter.19
  268.3 23.7 all-gather.31
  294.2 37.0 all-gather.29
  333.2 22.9 all-gather.33
  357.8 37.0 all-gather.39
  396.6 31.7 all-gather.21
  430.5 54.7 all-gather.19
  486.8 53.5 all-gather.37
  542.3 31.6 all-gather.23
  576.1 35.2 reduce-scatter.37
  613.6 34.2 reduce-scatter.35
  650.1 51.0 reduce-scatter.23
  703.3 51.7 reduce-scatter.21
  757.2 36.7 all-gather.35
  796.1 53.6 all-gather.25
  852.8 33.8 reduce-scatter.47
  890.2 40.2 reduce-scatter.45
  932.9 35.2 reduce-scatter.39
  971.9 120.4 all-reduce.29
  1094.6 52.2 reduce-scatter.25
  1150.8 42.1 reduce-scatter.43
  1197.1 42.4 reduce-scatter.41
  1243.5 62.9 reduce-scatter.31
  1311.0 62.9 reduce-scatter.29
  1378.0 40.2 reduce-scatter.27
where the time goes:
time: 1430 us
  waiting for transfers between devices  967 us (68%)
  matrix products  200 us (14%)
  blocking collectives  96.7 us (7%)
  other arithmetic  80.5 us (6%)
  local copies, waits for them, and re-layouts  57.9 us (4%)
  between operations  19.8 us (1%)
    reduce_scatter x4, waiting for transfers between devices, sum_rows(): lax.psum_scatter(jnp.dot(left_rows, right_weight, preferred_element_type=...  137 us
    all_gather x4, waiting for transfers between devices, gather_rows(): return lax.all_gather(normed, 'tensor', axis=0, tiled=True)  132 us
    all_gather x4, waiting for transfers between devices, gather_grads(): return lax.all_gather(branch_grad, 'tensor', axis=0, tiled=True)  129 us
    reduce_scatter x4, waiting for transfers between devices, back_rows(): lax.psum_scatter(jnp.einsum('sle,sde->ld', grad_stack, weight_stack, pref...  111 us
    unnamed x32, waiting for transfers between devices  110 us
    reduce_scatter x1, waiting for transfers between devices, on_device(): lax.psum_scatter(teach_parts[2], 'dp', scatter_dimension=0, tiled=True)  67.4 us
    reduce_scatter x1, waiting for transfers between devices, on_device(): lax.psum_scatter(teach_parts[3], 'dp', scatter_dimension=1, tiled=True)  66.9 us
    all_gather x2, waiting for transfers between devices, run_block(): lax.all_gather(proj_weight, 'dp', axis=1, tiled=True)  53.6 us
  transfers between devices with their start and end apart: 29, of which 25 were waited for; matrix products, arithmetic and copies ran while one was open for 22% of the time, Pallas kernels for 0%

commit v1 on v0

--- a/solution.py
+++ b/solution.py
@@ -7,6 +7,28 @@
 SPAN = 256
 epsilon = 1e-05
 negative = -1e30
+
+
+def joined_along(blocks, dim):
+    lengths = list(blocks.shape[1:])
+    lengths[dim] *= blocks.shape[0]
+    return jnp.moveaxis(blocks, 0, dim).reshape(lengths)
+
+
+def gather_around(value, axis, dim):
+    count = lax.axis_size(axis)
+    pairs = [(i, (i + 1) % count) for i in range(count)]
+    back = [(b, a) for a, b in pairs]
+    lower, upper = ([], [])
+    for step in range(count - 1):
+        if step % 2 == 0:
+            lower.append(lax.ppermute(lower[-1] if lower else value, axis, pairs))
+        else:
+            upper.append(lax.ppermute(upper[-1] if upper else value, axis, back))
+    blocks = jnp.stack([*lower[::-1], value, *upper])
+    shift = lax.axis_index(axis) - len(lower)
+    blocks = blocks[(jnp.arange(count) - shift) % count]
+    return joined_along(blocks, dim)
 
 
 def layer_norm(values, norm_gain, norm_shift):
@@ -147,7 +169,7 @@
     gathered = (
         lax.all_gather(qkv_weight, "dp", axis=1, tiled=True),
         lax.all_gather(out_weight, "dp", axis=1, tiled=True),
-        lax.all_gather(fc_weight, "dp", axis=0, tiled=True),
+        gather_around(fc_weight, "dp", 0),
         lax.all_gather(proj_weight, "dp", axis=1, tiled=True),
         lax.all_gather(attn_gain, "dp", axis=0, tiled=True),
         lax.all_gather(attn_shift, "dp", axis=0, tiled=True),

time: 1430 us -> 1380 us (0.965)
  waiting for transfers between devices: 967 us -> 874 us
  local copies, waits for them, and re-layouts: 57.9 us -> 81.4 us
  starting transfers between devices: 3.09 us -> 18.4 us
    all_gather x4, waiting for transfers between devices: 132 us -> 62.5 us  [gather_rows(): return lax.all_gather(normed, 'tensor', axis=0, tiled=True)]
    ppermute x0 -> x14, waiting for transfers between devices: none -> 44.3 us  [the longest x8 31.7 us: gather_around(): lower.append(lax.ppermute(lower[-1] if lower else value, axis, pairs))]
    all_gather x2 -> x0, waiting for transfers between devices: 36 us -> none  [run_block(): lax.all_gather(fc_weight, 'dp', axis=0, tiled=True)]
    all_gather x2, waiting for transfers between devices: 53.6 us -> 33.6 us  [run_block(): lax.all_gather(proj_weight, 'dp', axis=1, tiled=True)]
    unnamed x316 -> x348, local copies, waits for them, and re-layouts: 42 us -> 57.5 us
    ppermute x0 -> x14, starting transfers between devices: none -> 15.1 us  [the longest x6 14.3 us: gather_around(): upper.append(lax.ppermute(upper[-1] if upper else value, axis, back))]
    unnamed x32 -> x30, waiting for transfers between devices: 110 us -> 109 us
  transfers between devices with their start and end apart: 29 -> 41, of which waited for: 25 -> 28; matrix products, arithmetic and copies ran while one was open for 22% -> 24% of each run, Pallas kernels for 0% -> 0%
where the time goes in v1:
time: 1380 us; the launch traced here: 1370 us
  waiting for transfers between devices  874 us (63%)
  matrix products  198 us (14%)
  blocking collectives  96.7 us (7%)
  local copies, waits for them, and re-layouts  81.4 us (6%)
  other arithmetic  80.3 us (6%)
  between operations  20.5 us (1%)
  starting transfers between devices  18.4 us (1%)
    reduce_scatter x4, waiting for transfers between devices, sum_rows(): lax.psum_scatter(jnp.dot(left_rows, right_weight, preferred_element_type=...  138 us
    all_gather x4, waiting for transfers between devices, gather_grads(): return lax.all_gather(branch_grad, 'tensor', axis=0, tiled=True)  116 us
    reduce_scatter x4, waiting for transfers between devices, back_rows(): lax.psum_scatter(jnp.einsum('sle,sde->ld', grad_stack, weight_stack, pref...  111 us
    unnamed x30, waiting for transfers between devices  109 us
    reduce_scatter x1, waiting for transfers between devices, on_device(): lax.psum_scatter(teach_parts[2], 'dp', scatter_dimension=0, tiled=True)  67.3 us
    reduce_scatter x1, waiting for transfers between devices, on_device(): lax.psum_scatter(teach_parts[3], 'dp', scatter_dimension=1, tiled=True)  67.1 us
    all_gather x4, waiting for transfers between devices, gather_rows(): return lax.all_gather(normed, 'tensor', axis=0, tiled=True)  62.5 us
    unnamed x348, local copies, waits for them, and re-layouts  57.5 us
  transfers between devices with their start and end apart: 41, of which 28 were waited for; matrix products, arithmetic and copies ran while one was open for 24% of the time, Pallas kernels for 0%

profile of v1, /device:TPU:0, one launch (start us, length us, event | category | flops | bytes accessed | tf_op | source)
XLA Modules:
  0.0 1368.7 jit_solution(9108304256789837599)
XLA Ops:
  22.5 26.5 %all-reduce.27 = (bf16[1280]{0:T(1024)(128)(2,1)}, bf16[1280]{0:T(1024)(128)(2,1)}, bf16[1280]{0:T(1024)(128)(2,1)S(1)}, bf16[1280]{0:T(1024)(128)(2,1)S(1)}, bf...) all-reduce(bf16[1280]{0:T(1024)(128)(2,1)S(1)} %dynamic-update-slic, ...), channel_id=1, replica_groups=mesh['dp'=8,'tensor'=4] {'dp'}, use_global_device_ids=true, to_apply=%add.4 | all-reduce | flops 12288 | bytes 49152
  56.3 10.9 all_gather.82
  67.2 13.4 all_gather.94
  80.7 9.0 all_gather.95
  108.0 35.6 %all-gather.14.cloned.1.call-done = bf16[1024,1280]{1,0:T(8,128)(2,1)} async-done(((bf16[256,1280]{1,0:T(8,128)(2,1)}), bf16[1024,1280]{1,0:T(8,128)(2,1)}) %all-gather.14.cloned.1.call-update) | async-done | bytes 2621456 | tf_op jit(solution)/shard_map/all_gather | solution.py:124
  143.7 32.2 %all-gather.16.cloned.1.call-done = bf16[3,1280,384]{2,1,0:T(8,128)(2,1)} async-done(((bf16[3,160,384]{2,1,0:T(8,128)(2,1)}), bf16[3,1280,384]{2,1,0:T(8,128)(2,1)}) %all-gather.16.cloned.1.call-update) | async-done | bytes 2949136 | tf_op jit(solution)/shard_map/all_gather | solution.py:170
  175.9 6.0 fusion.47
  189.5 3.8 fusion.10
  200.5 3.8 fusion.11
  208.6 4.8 reduce-scatter.34.cloned.1.call-done
  219.5 47.1 %reduce-scatter.20.cloned.1.call-done = bf16[256,1280]{1,0:T(8,128)(2,1)} async-done(((bf16[1024,1280]{1,0:T(8,128)(2,1)}), bf16[256,1280]{1,0:T(8,128)(2,1)}) %reduce-scatter.20.cloned.1.call-update) | async-done | bytes 655376 | tf_op jit(solution)/shard_map/reduce_scatter | solution.py:132
  273.3 5.5 collective-permute-done.7
  284.8 8.5 collective-permute-done.11
  293.3 3.2 collective-permute-start.12
  296.6 4.1 collective-permute-done.12
  300.7 3.2 collective-permute-start.13
  309.4 5.3 collective-permute-done.1
  316.6 6.6 collective-permute-done.2
  327.7 11.5 collective-permute-done.3
  341.1 4.9 fusion.172
  346.0 26.8 %all-gather.34.cloned.1.call-done = bf16[1,1024,768]{2,1,0:T(8,128)(2,1)} async-done(((bf16[1,256,768]{2,1,0:T(8,128)(2,1)}), bf16[1,1024,768]{2,1,0:T(8,128)(2,1)}) %all-gather.34.cloned.1.call-update) | async-done | bytes 1572880 | tf_op jit(solution)/shard_map/all_gather | solution.py:128
  372.8 6.3 convert_reduce_fusion.4
  391.9 3.3 convolution_convert_fusion.4
  397.4 4.4 gather_fusion
  401.8 26.8 %all-gather.18.cloned.1.call-done = bf16[1024,1280]{1,0:T(8,128)(2,1)} async-done(((bf16[256,1280]{1,0:T(8,128)(2,1)}), bf16[1024,1280]{1,0:T(8,128)(2,1)}) %all-gather.18.cloned.1.call-update) | async-done | bytes 2621456 | tf_op jit(solution)/shard_map/all_gather | solution.py:124
  428.7 8.6 fusion.168
  437.2 46.5 %all-gather.32.cloned.1.call-done = bf16[1,1024,1280]{2,1,0:T(8,128)(2,1)} async-done(((bf16[1,256,1280]{2,1,0:T(8,128)(2,1)}), bf16[1,1024,1280]{2,1,0:T(8,128)(2,1)}) %all-gather.32.cloned.1.call-update) | async-done | bytes 2621456 | tf_op jit(solution)/shard_map/all_gather | solution.py:128
  483.7 33.6 %all-gather.20.cloned.1.call-done = bf16[1280,1280]{0,1:T(8,128)(2,1)} async-done(((bf16[1280,160]{0,1:T(8,128)(2,1)}), bf16[1280,1280]{0,1:T(8,128)(2,1)}) %all-gather.20.cloned.1.call-update) | async-done | bytes 3276816 | tf_op jit(solution)/shard_map/all_gather | solution.py:173
  517.3 10.7 convert_reduce_fusion.1
  529.5 4.9 convolution_convert_fusion.1
  534.5 9.8 convolution_convert_fusion.2
  544.5 10.2 reduce-scatter.38.cloned.1.call-done
  556.8 34.6 %reduce-scatter.36.cloned.1.call-done = bf16[256,768]{1,0:T(8,128)(2,1)} async-done(((bf16[1024,768]{1,0:T(8,128)(2,1)}), bf16[256,768]{1,0:T(8,128)(2,1)}) %reduce-scatter.36.cloned.1.call-update) | async-done | bytes 393232 | tf_op jit(solution)/shard_map/reduce_scatter | solution.py:132
  596.0 48.7 %reduce-scatter.24.cloned.1.call-done = bf16[256,1280]{1,0:T(8,128)(2,1)} async-done(((bf16[1024,1280]{1,0:T(8,128)(2,1)}), bf16[256,1280]{1,0:T(8,128)(2,1)}) %reduce-scatter.24.cloned.1.call-update) | async-done | bytes 655376 | tf_op jit(solution)/shard_map/reduce_scatter | solution.py:141
  647.0 51.6 %reduce-scatter.22.cloned.1.call-done = bf16[256,1280]{1,0:T(8,128)(2,1)} async-done(((bf16[1024,1280]{1,0:T(8,128)(2,1)}), bf16[256,1280]{1,0:T(8,128)(2,1)}) %reduce-scatter.22.cloned.1.call-update) | async-done | bytes 655376 | tf_op jit(solution)/shard_map/reduce_scatter | solution.py:132
  704.2 33.2 %all-gather.30.cloned.1.call-done = bf16[1024,768]{1,0:T(8,128)(2,1)} async-done(((bf16[256,768]{1,0:T(8,128)(2,1)}), bf16[1024,768]{1,0:T(8,128)(2,1)}) %all-gather.30.cloned.1.call-update) | async-done | bytes 1572880 | tf_op jit(solution)/shard_map/all_gather | solution.py:128
  743.1 4.3 multiply_reduce_fusion.3
  755.4 5.0 multiply_reduce_fusion.2
  760.7 5.6 multiply_convert_fusion.2
  773.8 4.8 reshape.545
  778.8 3.9 bitcast_convert_fusion.1
  783.2 10.0 all-gather.22.cloned.1.call-done
  796.3 6.0 fusion.4
  802.3 9.6 multiply_reduce_fusion
  811.9 6.3 multiply_reduce_fusion.1
  821.7 9.7 multiply_convert_fusion.1
  836.0 6.7 multiply_convert_fusion
  846.5 5.0 fusion.95
  854.1 8.4 convolution_bitcast_fusion
  862.5 9.8 copy.70
  872.4 7.8 bitcast_convert_fusion
  880.3 5.3 fusion.63
  885.9 4.8 fusion.174
  890.8 9.8 fusion.38
  900.7 8.9 fusion.170
  920.9 5.2 fusion.154
  930.3 105.2 %all-reduce.30.cloned.1.call-done = f32[3,1280,384]{2,0,1:T(4,128)} async-done(((f32[3,1280,384]{2,0,1:T(4,128)}), f32[3,1280,384]{2,0,1:T(4,128)}) %all-reduce.30.cloned.1.call-update) | async-done | bytes 5898256
  1037.8 52.3 %reduce-scatter.26.cloned.1.call-done = bf16[256,1280]{1,0:T(8,128)(2,1)} async-done(((bf16[1024,1280]{1,0:T(8,128)(2,1)}), bf16[256,1280]{1,0:T(8,128)(2,1)}) %reduce-scatter.26.cloned.1.call-update) | async-done | bytes 655376 | tf_op jit(solution)/shard_map/reduce_scatter | solution.py:141
  1093.6 25.6 %all-reduce.25 = (f32[1280]{0:T(1024)S(1)}, f32[1280]{0:T(1024)S(1)}, f32[2,384]{1,0:T(2,128)}, f32[1280]{0:T(1024)S(1)}, f32[1280]{0:T(1024)S(1)}, /*index=5*/f...) all-reduce(f32[1280]{0:T(1024)S(1)} %get-tuple-element.86, ...), channel_id=8, replica_groups=mesh['dp'=8,'tensor'=4] {'dp'}, use_global_device_ids=true, to_apply=%region_20.21.clone | all-reduce | flops 15488 | bytes 123904
  1122.2 11.3 all-reduce.26
  1136.2 46.7 %reduce-scatter.42.cloned.1.call-done = f32[96,768]{1,0:T(8,128)} async-done(((f32[768,768]{1,0:T(8,128)}), f32[96,768]{1,0:T(8,128)}) %reduce-scatter.42.cloned.1.call-update) | async-done | bytes 294928 | tf_op jit(solution)/shard_map/reduce_scatter | solution.py:383
  1182.9 67.1 %reduce-scatter.32.cloned.1.call-done = f32[1280,160]{0,1:T(8,128)} async-done(((f32[1280,1280]{0,1:T(8,128)}), f32[1280,160]{0,1:T(8,128)}) %reduce-scatter.32.cloned.1.call-update) | async-done | bytes 819216 | tf_op jit(solution)/shard_map/reduce_scatter | solution.py:374
  1250.0 67.3 %reduce-scatter.30.cloned.1.call-done = f32[160,1280]{1,0:T(8,128)} async-done(((f32[1280,1280]{1,0:T(8,128)}), f32[160,1280]{1,0:T(8,128)}) %reduce-scatter.30.cloned.1.call-update) | async-done | bytes 819216 | tf_op jit(solution)/shard_map/reduce_scatter | solution.py:373
  1317.2 44.1 %reduce-scatter.28.cloned.1.call-done = f32[384,160]{0,1:T(8,128)} async-done(((f32[384,1280]{0,1:T(8,128)}), f32[384,160]{0,1:T(8,128)}) %reduce-scatter.28.cloned.1.call-update) | async-done | bytes 245776 | tf_op jit(solution)/shard_map/reduce_scatter | solution.py:372
  (569 shorter events, 186.2 us)
Async XLA Ops:
  7.3 85.9 %all-gather.24.cloned.1.call-start = ((), (), s32[]{:S(2)}) async-start(), calls=%async_computation.27 | async-start | bytes 1966080 | tf_op jit(solution)/shard_map/all_gather | solution.py:124
  11.1 56.1 %copy-start.83 = (f32[256]{0:T(256)}, f32[256]{0:T(256)S(1)}, u32[]{:S(2)}) copy-start(f32[256]{0:T(256)S(1)} %broadcast_multiply_fusion.2) | copy-start | bytes 3076
  51.0 92.6 %all-gather.14.cloned.1.call-start = ((), (), s32[]{:S(2)}) async-start(), calls=%async_computation.15 | async-start | bytes 3276800 | tf_op jit(solution)/shard_map/all_gather | solution.py:124
  54.0 121.9 %all-gather.16.cloned.1.call-start = ((), (), s32[]{:S(2)}) async-start(), calls=%async_computation.16 | async-start | bytes 3317760 | tf_op jit(solution)/shard_map/all_gather | solution.py:170
  54.7 158.6 %reduce-scatter.34.cloned.1.call-start = ((), (), s32[]{:S(2)}) async-start(), calls=%async_computation.28 | async-start | bytes 1966080 | tf_op jit(solution)/shard_map/reduce_scatter | solution.py:132
  90.0 114.4 %copy-start.116 = (f32[384]{0:T(512)}, f32[384]{0:T(512)S(1)}, u32[]{:S(2)}) copy-start(f32[384]{0:T(512)S(1)} %mul.401) | copy-start | bytes 4612
  105.6 76.2 %copy-start.57 = (bf16[3,64,512]{2,1,0:T(8,128)(2,1)}, bf16[3,64,512]{2,1,0:T(8,128)(2,1)S(1)}, u32[]{:S(2)}) copy-start(bf16[3,64,512]{2,1,0:T(8,128)(2,1)S(1)} %fusion.100) | copy-start | bytes 589828
  107.5 159.1 %reduce-scatter.20.cloned.1.call-start = ((), (), s32[]{:S(2)}) async-start(), calls=%async_computation.17 | async-start | bytes 3276800 | tf_op jit(solution)/shard_map/reduce_scatter | solution.py:132
  208.4 132.6 %all-gather.26.cloned.1.call-start = ((), (), s32[]{:S(2)}) async-start(), calls=%async_computation.29 | async-start | bytes 1966080 | tf_op jit(solution)/shard_map/all_gather | solution.py:124
  217.8 128.2 %all-gather.28.cloned.1.call-start = ((), (), s32[]{:S(2)}) async-start(), calls=%async_computation.30 | async-start | bytes 1327104 | tf_op jit(solution)/shard_map/all_gather | solution.py:173
  218.6 154.3 %all-gather.34.cloned.1.call-start = ((), (), s32[]{:S(2)}) async-start(), calls=%async_computation.38 | async-start | bytes 1966080 | tf_op jit(solution)/shard_map/all_gather | solution.py:128
  219.3 209.4 %all-gather.18.cloned.1.call-start = ((), (), s32[]{:S(2)}) async-start(), calls=%async_computation.18 | async-start | bytes 3276800 | tf_op jit(solution)/shard_map/all_gather | solution.py:124
  219.4 59.3 %copy-start.60 = (bf16[160,1280]{1,0:T(8,128)(2,1)S(1)}, bf16[160,1280]{1,0:T(8,128)(2,1)}, u32[]{:S(2)}) copy-start(bf16[160,1280]{1,0:T(8,128)(2,1)} %param.40) | copy-start | bytes 1228804
  219.5 77.1 %copy-start.115 = (bf16[768]{0:T(1024)(128)(2,1)S(1)}, bf16[768]{0:T(1024)(128)(2,1)}, u32[]{:S(2)}) copy-start(bf16[768]{0:T(1024)(128)(2,1)} %param.55) | copy-start | bytes 4612
  219.5 77.1 %copy-start.106 = (bf16[1280]{0:T(1024)(128)(2,1)S(1)}, bf16[1280]{0:T(1024)(128)(2,1)}, u32[]{:S(2)}) copy-start(bf16[1280]{0:T(1024)(128)(2,1)} %param.41) | copy-start | bytes 7684
  271.8 211.9 %all-gather.32.cloned.1.call-start = ((), (), s32[]{:S(2)}) async-start(), calls=%async_computation.37 | async-start | bytes 3276800 | tf_op jit(solution)/shard_map/all_gather | solution.py:128
  272.4 244.9 %all-gather.20.cloned.1.call-start = ((), (), s32[]{:S(2)}) async-start(), calls=%async_computation.19 | async-start | bytes 3686400 | tf_op jit(solution)/shard_map/all_gather | solution.py:173
  273.1 281.6 %reduce-scatter.38.cloned.1.call-start = ((), (), s32[]{:S(2)}) async-start(), calls=%async_computation.32 | async-start | bytes 1966080 | tf_op jit(solution)/shard_map/reduce_scatter | solution.py:141
  273.2 5.5 collective-permute-start.7
  278.7 6.1 collective-permute-start.8
  278.7 25.2 %collective-permute-start = (bf16[160,1280]{1,0:T(8,128)(2,1)S(1)}, bf16[160,1280]{1,0:T(8,128)(2,1)}, u32[]{:S(2)}, u32[]{:S(2)}) collective-permute-start(bf16[160,1280]{1,0:T(8,128)(2,1)S(1)} %copy-done.60), channel_id=1, source_target_pairs={{0,4},{4,8},{8,12},{12,16},{16,20},{20,24},{24,28},{28,0},{1,5},{5... | collective-permute-start | bytes 1228808 | tf_op jit(solution)/shard_map/ppermute | solution.py:25
  279.4 24.5 %collective-permute-start.4 = (bf16[160,1280]{1,0:T(8,128)(2,1)S(1)}, bf16[160,1280]{1,0:T(8,128)(2,1)S(1)}, u32[]{:S(2)}, u32[]{:S(2)}) collective-permute-start(bf16[160,1280]{1,0:T(8,128)(2,1)S(1)} %copy-done.60), channel_id=1, source_target_pairs={{4,0},{8,4},{12,8},{16,12},{20,16},{24,20},{28,24},{0,28},{5,1},{9... | collective-permute-start | bytes 1228808 | tf_op jit(solution)/shard_map/ppermute | solution.py:27
  281.4 11.9 collective-permute-start.11
  284.8 11.7 collective-permute-start.9
  293.3 7.4 collective-permute-start.12
  296.5 10.1 collective-permute-start.10
  296.6 95.3 %copy-start.113 = (f32[768]{0:T(1024)}, f32[768]{0:T(1024)S(1)}, u32[]{:S(2)}) copy-start(f32[768]{0:T(1024)S(1)} %convert_element_type.331) | copy-start | bytes 9220
  296.6 237.9 %copy-start.104 = (f32[1280]{0:T(1024)}, f32[1280]{0:T(1024)S(1)}, u32[]{:S(2)}) copy-start(f32[1280]{0:T(1024)S(1)} %convert_element_type.289) | copy-start | bytes 15364
  300.7 22.5 %collective-permute-start.13 = (bf16[96,768]{1,0:T(8,128)(2,1)S(1)}, bf16[96,768]{1,0:T(8,128)(2,1)S(1)}, u32[]{:S(2)}, u32[]{:S(2)}) collective-permute-start(bf16[96,768]{1,0:T(8,128)(2,1)S(1)} %collective-permute-done.12), channel_id=1, source_target_pairs={{4,0},{8,4},{12,8},{16,12},{20,16},{24,20},{28,24},{0,28},{5,1},{9... | collective-permute-start | bytes 442376 | tf_op jit(solution)/shard_map/ppermute | solution.py:27
  303.9 10.7 collective-permute-start.1
  303.9 21.0 %collective-permute-start.5 = (bf16[160,1280]{1,0:T(8,128)(2,1)S(1)}, bf16[160,1280]{1,0:T(8,128)(2,1)}, u32[]{:S(2)}, u32[]{:S(2)}) collective-permute-start(bf16[160,1280]{1,0:T(8,128)(2,1)S(1)} %collective-permute-done.4), channel_id=1, source_target_pairs={{4,0},{8,4},{12,8},{16,12},{20,16},{24,20},{28,24},{0,28},{5,1},{9... | collective-permute-start | bytes 1228808 | tf_op jit(solution)/shard_map/ppermute | solution.py:27
  314.6 8.5 collective-permute-start.2
  323.2 16.1 %collective-permute-start.3 = (bf16[160,1280]{1,0:T(8,128)(2,1)}, bf16[160,1280]{1,0:T(8,128)(2,1)}, u32[]{:S(2)}, u32[]{:S(2)}) collective-permute-start(bf16[160,1280]{1,0:T(8,128)(2,1)} %collective-permute-done.2), channel_id=1, source_target_pairs={{0,4},{4,8},{8,12},{12,16},{16,20},{20,24},{24,28},{28,0},{1,5},{5... | collective-permute-start | bytes 1228808 | tf_op jit(solution)/shard_map/ppermute | solution.py:25
  324.9 70.7 %collective-permute-start.6 = (bf16[160,1280]{1,0:T(8,128)(2,1)}, bf16[160,1280]{1,0:T(8,128)(2,1)}, u32[]{:S(2)}, u32[]{:S(2)}) collective-permute-start(bf16[160,1280]{1,0:T(8,128)(2,1)} %collective-permute-done.5), channel_id=1, source_target_pairs={{4,0},{8,4},{12,8},{16,12},{20,16},{24,20},{28,24},{0,28},{5,1},{9... | collective-permute-start | bytes 1228808 | tf_op jit(solution)/shard_map/ppermute | solution.py:27
  382.9 208.5 %reduce-scatter.36.cloned.1.call-start = ((), (), s32[]{:S(2)}) async-start(), calls=%async_computation.31 | async-start | bytes 1966080 | tf_op jit(solution)/shard_map/reduce_scatter | solution.py:132
  395.2 249.5 %reduce-scatter.24.cloned.1.call-start = ((), (), s32[]{:S(2)}) async-start(), calls=%async_computation.21 | async-start | bytes 3276800 | tf_op jit(solution)/shard_map/reduce_scatter | solution.py:141
  534.4 164.2 %reduce-scatter.22.cloned.1.call-start = ((), (), s32[]{:S(2)}) async-start(), calls=%async_computation.20 | async-start | bytes 3276800 | tf_op jit(solution)/shard_map/reduce_scatter | solution.py:132
  544.3 100.3 %copy-start.11 = (bf16[256,1280]{1,0:T(8,128)(2,1)S(1)}, bf16[256,1280]{1,0:T(8,128)(2,1)}, u32[]{:S(2)}) copy-start(bf16[256,1280]{1,0:T(8,128)(2,1)} %reduce-scatter.20.cloned.1.call-done) | copy-start | bytes 1966084
  544.3 193.1 %all-gather.30.cloned.1.call-start = ((), (), s32[]{:S(2)}) async-start(), calls=%async_computation.33 | async-start | bytes 1966080 | tf_op jit(solution)/shard_map/all_gather | solution.py:128
  593.7 107.8 %copy-start.101 = (f32[256]{0:T(256)}, f32[256]{0:T(256)S(1)}, u32[]{:S(2)}) copy-start(f32[256]{0:T(256)S(1)} %negate_multiply_fusion.1) | copy-start | bytes 3076
  595.9 197.2 %all-gather.22.cloned.1.call-start = ((), (), s32[]{:S(2)}) async-start(), calls=%async_computation.22 | async-start | bytes 3276800 | tf_op jit(solution)/shard_map/all_gather | solution.py:128
  704.1 211.7 %reduce-scatter.48.cloned.1.call-start = ((), (), s32[]{:S(2)}) async-start(), calls=%async_computation.40 | async-start | bytes 884736
  760.4 157.0 %reduce-scatter.46.cloned.1.call-start = ((), (), s32[]{:S(2)}) async-start(), calls=%async_computation.39 | async-start | bytes 2211840
  778.7 140.7 %reduce-scatter.40.cloned.1.call-start = ((), (), s32[]{:S(2)}) async-start(), calls=%async_computation.34 | async-start | bytes 1966080 | tf_op jit(solution)/shard_map/reduce_scatter | solution.py:141
  782.7 252.8 %all-reduce.30.cloned.1.call-start = ((), (), s32[]{:S(2)}) async-start(), calls=%async_computation.41 | async-start | bytes 15728640
  872.4 217.7 %reduce-scatter.26.cloned.1.call-start = ((), (), s32[]{:S(2)}) async-start(), calls=%async_computation.23 | async-start | bytes 3276800 | tf_op jit(solution)/shard_map/reduce_scatter | solution.py:141
  880.3 256.0 %reduce-scatter.44.cloned.1.call-start = ((), (), s32[]{:S(2)}) async-start(), calls=%async_computation.36 | async-start | bytes 2654208 | tf_op jit(solution)/shard_map/reduce_scatter | solution.py:384
  885.6 297.2 %reduce-scatter.42.cloned.1.call-start = ((), (), s32[]{:S(2)}) async-start(), calls=%async_computation.35 | async-start | bytes 2654208 | tf_op jit(solution)/shard_map/reduce_scatter | solution.py:383
  890.7 359.2 %reduce-scatter.32.cloned.1.call-start = ((), (), s32[]{:S(2)}) async-start(), calls=%async_computation.26 | async-start | bytes 7372800 | tf_op jit(solution)/shard_map/reduce_scatter | solution.py:374
  900.6 416.6 %reduce-scatter.30.cloned.1.call-start = ((), (), s32[]{:S(2)}) async-start(), calls=%async_computation.25 | async-start | bytes 7372800 | tf_op jit(solution)/shard_map/reduce_scatter | solution.py:373
  909.6 451.8 %reduce-scatter.28.cloned.1.call-start = ((), (), s32[]{:S(2)}) async-start(), calls=%async_computation.24 | async-start | bytes 2211840 | tf_op jit(solution)/shard_map/reduce_scatter | solution.py:372
  929.7 160.3 %copy-start.63 = (f32[1280]{0:T(1024)S(1)}, f32[1280]{0:T(1024)}, u32[]{:S(2)}) copy-start(f32[1280]{0:T(1024)} %copy-done.62) | copy-start | bytes 15364
  929.8 160.3 %copy-start.86 = (f32[256]{0:T(256)S(1)}, f32[256]{0:T(256)}, u32[]{:S(2)}) copy-start(f32[256]{0:T(256)} %copy-done.85) | copy-start | bytes 3076
  930.2 161.5 %copy-start.100 = (f32[256]{0:T(256)S(1)}, f32[256]{0:T(256)}, u32[]{:S(2)}) copy-start(f32[256]{0:T(256)} %copy-done.99) | copy-start | bytes 3076
  930.2 161.5 %copy-start.94 = (f32[256]{0:T(256)S(1)}, f32[256]{0:T(256)}, u32[]{:S(2)}) copy-start(f32[256]{0:T(256)} %copy-done.93) | copy-start | bytes 3076
  930.2 163.3 %copy-start.87 = (f32[1280]{0:T(1024)S(1)}, f32[1280]{0:T(1024)}, u32[]{:S(2)}) copy-start(f32[1280]{0:T(1024)} %get-tuple-element.84) | copy-start | bytes 15364
  930.2 163.3 %copy-start.88 = (f32[1280]{0:T(1024)S(1)}, f32[1280]{0:T(1024)}, u32[]{:S(2)}) copy-start(f32[1280]{0:T(1024)} %get-tuple-element.92) | copy-start | bytes 15364
  930.2 163.3 %copy-start.91 = (f32[768]{0:T(1024)S(1)}, f32[768]{0:T(1024)}, u32[]{:S(2)}) copy-start(f32[768]{0:T(1024)} %get-tuple-element.88) | copy-start | bytes 9220
  930.2 163.3 %copy-start.92 = (f32[768]{0:T(1024)S(1)}, f32[768]{0:T(1024)}, u32[]{:S(2)}) copy-start(f32[768]{0:T(1024)} %get-tuple-element.95) | copy-start | bytes 9220
  930.2 163.3 %copy-start.103 = (f32[1280]{0:T(1024)S(1)}, f32[1280]{0:T(1024)}, u32[]{:S(2)}) copy-start(f32[1280]{0:T(1024)} %get-tuple-element.162) | copy-start | bytes 15364
  930.3 163.3 %copy-start.108 = (f32[768]{0:T(1024)S(1)}, f32[768]{0:T(1024)}, u32[]{:S(2)}) copy-start(f32[768]{0:T(1024)} %get-tuple-element.172) | copy-start | bytes 9220
  930.3 203.2 %copy-start.15 = (f32[256,1280]{1,0:T(8,128)S(1)}, f32[256,1280]{1,0:T(8,128)}, u32[]{:S(2)}) copy-start(f32[256,1280]{1,0:T(8,128)} %copy-done.14) | copy-start | bytes 3932164
  930.3 203.2 %copy-start.24 = (bf16[1,256,1280]{2,1,0:T(8,128)(2,1)S(1)}, bf16[1,256,1280]{2,1,0:T(8,128)(2,1)}, u32[]{:S(2)}) copy-start(bf16[1,256,1280]{2,1,0:T(8,128)(2,1)} %param.31) | copy-start | bytes 1966084
  930.3 203.2 %copy-start.96 = (f32[256]{0:T(256)S(1)}, f32[256]{0:T(256)}, u32[]{:S(2)}) copy-start(f32[256]{0:T(256)} %copy-done.95) | copy-start | bytes 3076
  (121 other events, 1639.1 us)
Sparse Core Ops, SparseCore 0:
  51.2 36.5 all-gather.23
  89.9 53.6 all-gather.13
  145.6 30.2 all-gather.15
  178.0 35.2 reduce-scatter.33
  215.5 51.0 reduce-scatter.19
  268.6 36.7 all-gather.25
  307.3 26.8 all-gather.27
  335.7 37.0 all-gather.33
  375.0 53.6 all-gather.17
  430.1 53.5 all-gather.31
  485.6 31.6 all-gather.19
  519.4 35.2 reduce-scatter.37
  557.0 34.2 reduce-scatter.35
  593.5 51.0 reduce-scatter.23
  646.8 51.7 reduce-scatter.21
  700.6 36.7 all-gather.29
  739.4 53.6 all-gather.21
  796.1 33.8 reduce-scatter.47
  833.4 40.2 reduce-scatter.45
  876.0 35.2 reduce-scatter.39
  915.0 120.4 all-reduce.29
  1037.8 52.2 reduce-scatter.25
  1094.0 42.1 reduce-scatter.43
  1140.4 42.4 reduce-scatter.41
  1186.9 63.0 reduce-scatter.31
  1254.2 62.9 reduce-scatter.29
  1321.1 40.2 reduce-scatter.27
